TPU v7x, 32 devices: a whole 2x2x4 slice. The times are simulated.
32 devices in a mesh: groups: 2 (over x), rows: 16 (over z, y, core).
Axes of the slice: x: 2, y: 2, z: 4, core: 2. Of those that a mesh axis runs over, the one named last changes fastest.
Arguments:
- in_acts: bfloat16 [512, 14336], P(('groups', 'rows')), parts along dimension 0, may hold values from -6 to 6
- out_grads: bfloat16 [512, 4096], P(('groups', 'rows')), parts along dimension 0, may hold values from -6 to 6
- in_projection: bfloat16 [128, 14336], replicated, may hold values from -0.046875 to 0.046875
- out_projection: bfloat16 [128, 4096], replicated, may hold values from -0.09375 to 0.09375
- inverse: bfloat16 [16384, 16384], P('rows'), as said below
- stored_rows: bfloat16 [1536, 16384], P(('groups', 'rows')), parts along dimension 0, may hold values from -0.0078125 to 0.0078125
- query_ids: int32 [512], P(('groups', 'rows')), parts along dimension 0, may hold values from 0 to 15, never falling along the last dimension, each value on 1 to 32 neighbouring positions
- example_ids: int32 [32, 48], P(('groups', 'rows')), parts along dimension 0, may hold values from 0 to 15, never falling along the last dimension, each value on 1 to 8 neighbouring positions
Outputs:
- example_scores: float32 [512, 16], P(('groups', 'rows')), parts along dimension 0
There are 2 independent parts, one for each index of `groups`. A program takes and returns all parts, laid end to end along the dimension named above; an argument that names none is the same for every part. Nothing has to cross between parts.
Inputs may be any that keep to these rules, and one draw needn't show every extreme that they name: `query_ids`: tokens of one query stand together, queries in increasing order; a query may span several devices. `example_ids`: within each block, rows of one example stand together in increasing order, each example with at least one row. `inverse`: the matrix is exactly symmetric.
All inputs are finite; a program needn't handle non-finite values.
Results may differ from a plain program's by a relative error of at most 0.0057.
Values may be sent and summed in bfloat16 or wider, within the bound.
No kernel may reach another device: no remote copies, remote signals or barrier semaphores. Data moves between devices by JAX's collectives and lax.ppermute only.
A program may use at most 128 MiB of HBM per device.

v0:
```python
import functools

import jax
import jax.numpy as jnp
from jax import lax
from jax.experimental import pallas as pl
from jax.experimental.pallas import tpu as pltpu
from jax.sharding import PartitionSpec as P


LANES = 128
QRY_DEV = 1
EX_DEV = 16
NT = (((1,), (1,)), ((), ()))
VMEM = pl.BlockSpec(memory_space=pltpu.VMEM)
ANY = pl.BlockSpec(memory_space=pl.ANY)
PROJECT_VMEM = 56_543_328


def chunk_of(total, most):
    size = most
    while total % size:
        size //= 2
    return size


def round_up(n, m):
    return -(-n // m) * m


def portions(total, weights):
    unit = 2 * LANES
    cuts = [total * sum(weights[:k]) // sum(weights) // unit * unit for k in range(len(weights))]
    cuts.append(total)
    return [(lo, hi - lo) for lo, hi in zip(cuts, cuts[1:])]


def project_kernel(acts, grads, in_w, out_w, raw, acts_v, grads_v, in_v, out_v, sem, *, steps):
    copies = []
    for n, (own, other) in enumerate(steps):
        parts = ((grads, grads_v, other), (out_w, out_v, other), (acts, acts_v, own), (in_w, in_v, own))
        copies.append(
            [
                pltpu.make_async_copy(
                    src.at[:, pl.ds(start, size)], dst.at[:, pl.ds(start, size)], sem.at[n, k]
                )
                for k, (src, dst, (start, size)) in enumerate(parts)
            ]
        )
    for step in copies:
        for copy in step:
            copy.start()

    def product(x, w, start, size):
        return lax.dot_general(
            x[:, start : start + size],
            w[:, start : start + size],
            NT,
            preferred_element_type=jnp.float32,
        )

    kin = in_w.shape[0]
    in_sum, out_sum = [], []
    for n, ((start, size), other) in enumerate(steps):
        for copy in copies[n]:
            copy.wait()
        half = size // 2
        in_sum += [
            product(acts_v, in_v, start, half),
            product(acts_v, in_v, start + half, size - half),
        ]
        out_sum.append(product(grads_v, out_v, *other))
    raw[:, :kin] = sum(in_sum[1:], in_sum[0]).astype(jnp.bfloat16)
    raw[:, kin:] = sum(out_sum[1:], out_sum[0]).astype(jnp.bfloat16)


def mark_kernel(raw, ids, tok):
    tokens, done = raw.shape
    row = lax.broadcasted_iota(jnp.int32, (tokens, tokens), 0)
    col = lax.broadcasted_iota(jnp.int32, (tokens, tokens), 1)
    mine = jnp.sum(jnp.where(row == col, ids[...], 0), axis=1, keepdims=True)
    query = lax.broadcasted_iota(jnp.int32, (tokens, tok.shape[1] - done), 1)
    tok[:, :done] = raw[...]
    tok[:, done:] = jnp.where(query == mine, 1.0, 0.0).astype(jnp.bfloat16)


def project(acts, grads, in_w, out_w, ids, queries):
    tokens, ff = acts.shape
    steps = list(zip(portions(ff, (2, 2, 2, 1)), portions(grads.shape[1], (1, 1, 1, 1))))
    width = in_w.shape[0] + out_w.shape[0]
    raw = pl.pallas_call(
        functools.partial(project_kernel, steps=steps),
        in_specs=[ANY] * 4,
        out_specs=VMEM,
        out_shape=jax.ShapeDtypeStruct((tokens, width), jnp.bfloat16),
        scratch_shapes=[
            pltpu.VMEM(acts.shape, acts.dtype),
            pltpu.VMEM(grads.shape, grads.dtype),
            pltpu.VMEM(in_w.shape, in_w.dtype),
            pltpu.VMEM(out_w.shape, out_w.dtype),
            pltpu.SemaphoreType.DMA((len(steps), 4)),
        ],
        compiler_params=pltpu.CompilerParams(vmem_limit_bytes=PROJECT_VMEM),
        name="project",
    )(acts, grads, in_w, out_w)
    return pl.pallas_call(
        mark_kernel,
        in_specs=[VMEM, VMEM],
        out_specs=VMEM,
        out_shape=jax.ShapeDtypeStruct(
            (tokens, width + round_up(queries, LANES)), jnp.bfloat16
        ),
        compiler_params=pltpu.CompilerParams(vmem_limit_bytes=2 << 20),
        cost_estimate=pl.CostEstimate(
            flops=10**11, bytes_accessed=10**8, transcendentals=0
        ),
        name="mark",
    )(raw, ids)


def precond_kernel(tok, inverse, out, out_t, member_t, *acc, kin, kout, per, fold, queries):
    out_t[...] = tok[:, kin : kin + kout].astype(jnp.float32).T.astype(jnp.bfloat16)
    member_t[...] = (
        tok[:, kin + kout :].astype(jnp.float32).T[:queries].astype(jnp.bfloat16)
    )

    def grads(first):
        o = out_t[pl.ds(first, per), :]
        weighted = (o[:, None, :] * member_t[...][None, :, :]).reshape(per * queries, o.shape[1])
        g = jnp.dot(weighted, tok[:, :kin], preferred_element_type=jnp.float32)
        g = g.astype(jnp.bfloat16)
        return [g[k * queries : (k + 1) * queries] for k in range(per)]

    def product(first):
        g = []
        for n in range(fold):
            g += grads(first + n * per)
        start = first * kin if isinstance(first, int) else pl.multiple_of(first * kin, kin)
        block = inverse[:, pl.ds(start, fold * per * kin)]
        return lax.dot_general(
            jnp.concatenate(g, axis=1), block, NT, preferred_element_type=jnp.float32
        )

    if not acc:
        out[...] = product(0).astype(jnp.bfloat16)
        return
    total = acc[0]
    total[...] = jnp.zeros_like(total)

    def step(s):
        total[...] += product(s * (fold * per))

    pl.loop(0, kout // (fold * per))(step)
    out[...] = total[...].astype(jnp.bfloat16)


def precondition(tok, inverse, kin, kout, queries):
    rows, coords = inverse.shape
    tokens = tok.shape[0]
    per = chunk_of(kout, max(8, (1 << 16) // (queries * tokens)))
    fold = chunk_of(kout // per, max(1, (1 << 18) // (per * queries * tokens) * 2))
    scratch = [
        pltpu.VMEM((kout, tokens), jnp.bfloat16),
        pltpu.VMEM((queries, tokens), jnp.bfloat16),
    ]
    if fold * per < kout:
        scratch.append(pltpu.VMEM((queries, rows), jnp.float32))
    return pl.pallas_call(
        functools.partial(
            precond_kernel, kin=kin, kout=kout, per=per, fold=fold, queries=queries
        ),
        in_specs=[VMEM, VMEM],
        out_specs=VMEM,
        out_shape=jax.ShapeDtypeStruct((queries, rows), jnp.bfloat16),
        scratch_shapes=scratch,
        compiler_params=pltpu.CompilerParams(vmem_limit_bytes=16 << 20),
        cost_estimate=pl.CostEstimate(
            flops=2 * queries * rows * coords,
            bytes_accessed=2 * rows * coords,
            transcendentals=0,
        ),
        name="precondition",
    )(tok, inverse)


def example_member(ids, examples):
    example = lax.broadcasted_iota(jnp.int32, (examples, ids.shape[1]), 0)
    return jnp.where(example == ids[...], 1.0, 0.0)


def near_kernel(*refs, near_masks, far_masks, axis):
    *held, stored, ids, part, sums = refs
    me = lax.axis_index(axis)
    rows, examples = held[0].shape[2], part.shape[0]
    member = example_member(ids, examples)
    scores = jnp.zeros((stored.shape[0], part.shape[1]), jnp.float32)
    blocks = [ref.at[n] for ref in held for n in range(ref.shape[0])]
    for block, mask in zip(blocks, near_masks, strict=True):
        start = pl.multiple_of((me ^ mask) * rows, rows)
        scores += lax.dot_general(
            stored[:, pl.ds(start, rows)], block[...], NT, preferred_element_type=jnp.float32
        )
    part[...] = jnp.dot(
        member, scores, precision=lax.Precision.HIGHEST, preferred_element_type=jnp.float32
    )
    for n, mask in enumerate(far_masks):
        start = pl.multiple_of((me ^ mask) * rows, rows)
        total = jnp.dot(
            member.astype(jnp.bfloat16),
            stored[:, pl.ds(start, rows)],
            preferred_element_type=jnp.float32,
        )
        high = total.astype(jnp.bfloat16)
        sums[:examples, n * rows : (n + 1) * rows] = high
        sums[examples:, n * rows : (n + 1) * rows] = (
            total - high.astype(jnp.float32)
        ).astype(jnp.bfloat16)


def far_kernel(far, part, sums, out):
    rows, examples = far.shape[2], out.shape[0]
    total = jnp.zeros((2 * examples, out.shape[1]), jnp.float32)
    for n in range(far.shape[0]):
        total += lax.dot_general(
            sums[:, n * rows : (n + 1) * rows], far[n], NT, preferred_element_type=jnp.float32
        )
    out[...] = part[...] + total[:examples] + total[examples:]


def score_near(held, stored, ids, near_masks, far_masks):
    _, queries, rows = held[0].shape
    return pl.pallas_call(
        functools.partial(
            near_kernel, near_masks=near_masks, far_masks=far_masks, axis="rows"
        ),
        in_specs=[VMEM] * (len(held) + 2),
        out_specs=[VMEM] * 2,
        out_shape=[
            jax.ShapeDtypeStruct((EX_DEV, queries), jnp.float32),
            jax.ShapeDtypeStruct((2 * EX_DEV, len(far_masks) * rows), jnp.bfloat16),
        ],
        compiler_params=pltpu.CompilerParams(vmem_limit_bytes=8 << 20),
        cost_estimate=pl.CostEstimate(
            flops=stored.size * queries, bytes_accessed=stored.size, transcendentals=0
        ),
        name="score_near",
    )(*held, stored, ids)


def score_far(far, part, sums):
    return pl.pallas_call(
        far_kernel,
        in_specs=[VMEM] * 3,
        out_specs=VMEM,
        out_shape=jax.ShapeDtypeStruct(part.shape, jnp.float32),
        compiler_params=pltpu.CompilerParams(vmem_limit_bytes=8 << 20),
        cost_estimate=pl.CostEstimate(
            flops=2 * sums.size * part.shape[1], bytes_accessed=2 * sums.size, transcendentals=0
        ),
        name="score_far",
    )(far, part, sums)


def rounds_of(n):
    bits = []
    bit = n // 2
    while bit > 1:
        bits.append(bit)
        bit //= 2
    rounds = [[bits[0] | 1]] if bits else []
    for k in range(1, len(bits), 2):
        pair = bits[k : k + 2]
        rounds.append([m | 1 for m in ([sum(pair)] if len(pair) == 2 else []) + pair])
    return rounds + [[1]]


def swap(x, mask, n):
    return lax.ppermute(x, "rows", [(i, i ^ mask) for i in range(n)])


def spread(x, held, masks, n):
    pieces = [x] + [swap(x, mask, n) for mask in masks]
    held = held + [h ^ mask for mask in masks for h in held]
    return jnp.concatenate(pieces, axis=0), held


def on_device(
    in_acts, out_grads, in_projection, out_projection, inverse, stored_rows, query_ids, example_ids
):
    n = lax.axis_size("rows")
    queries = QRY_DEV * n
    kin, kout = in_projection.shape[0], out_projection.shape[0]
    tok = project(
        in_acts, out_grads, in_projection, out_projection, query_ids[None, :], queries
    )
    *rounds, (last,) = rounds_of(n)
    for masks in rounds:
        tok, _ = spread(tok, [0], masks, n)
    tok = jnp.concatenate([tok, swap(tok, last, n)], axis=0)
    near, held = precondition(tok, inverse, kin, kout, queries)[None], [0]
    for masks in rounds[:-1]:
        near, held = spread(near, held, masks, n)
    masks = rounds[-1]
    pieces = [swap(near, mask, n) for mask in masks]
    first = len(masks) // 2
    early = jnp.concatenate([near] + pieces[:first], axis=0)
    late = jnp.concatenate(pieces[first:], axis=0)
    early_held = held + [h ^ mask for mask in masks[:first] for h in held]
    late_held = [h ^ mask for mask in masks[first:] for h in held]
    across = swap(early, last, n)
    far = swap(late, last, n)
    part, sums = score_near(
        [early, late, across],
        stored_rows,
        example_ids,
        early_held + late_held + [h ^ last for h in early_held],
        [h ^ last for h in late_held],
    )
    return score_far(far, part, sums)


def solution(mesh):
    placed = (
        P(("groups", "rows"), None),
        P(("groups", "rows"), None),
        P(),
        P(),
        P("rows", None),
        P(("groups", "rows"), None),
        P(("groups", "rows")),
        P(("groups", "rows"), None),
    )

    return jax.shard_map(
        on_device,
        mesh=mesh,
        in_specs=placed,
        out_specs=P(("groups", "rows"), None),
        check_vma=False,
    )
```

profile of v0, /device:TPU:0, one launch (start us, length us, event | category | flops | bytes accessed | tf_op | source)
XLA Modules:
  0.0 39.1 jit_solution(12166437864595916357)
XLA Ops:
  0.0 3.7 %project.1.raw = bf16[16,256]{1,0:T(8,128)(2,1)S(1)} custom-call(bf16[16,14336]{1,0:T(8,128)(2,1)} %acts.1, bf16[16,4096]{1,0:T(8,128)(2,1)} %grads.1, bf16[128,14336]{1,0:T(8,128)(2,1)} %in_w.1, bf16[128,4096]{1,0:T(8,128)(2,1)} %out_w.1), custom_call_target="tpu_custom_call" | custom-call | tf_op jit(solution)/shard_map/project/pallas_call | solution.py:91
  3.9 3.5 %collective-permute-start = (bf16[16,384]{1,0:T(8,128)(2,1)S(1)}, bf16[16,384]{1,0:T(8,128)(2,1)S(1)}, u32[]{:S(2)}, u32[]{:S(2)}) collective-permute-start(bf16[16,384]{1,0:T(8,128)(2,1)S(1)} %mark.1), channel_id=1, source_target_pairs={{0,9},{1,8},{2,11},{3,10},{4,13},{5,12},{6,15},{7,14},{8,1},{9,0},... | collective-permute-start | bytes 36872 | tf_op jit(solution)/shard_map/ppermute | solution.py:278
  7.5 1.4 %collective-permute-done = bf16[16,384]{1,0:T(8,128)(2,1)S(1)} collective-permute-done((bf16[16,384]{1,0:T(8,128)(2,1)S(1)}, bf16[16,384]{1,0:T(8,128)(2,1)S(1)}, u32[]{:S(2)}, u32[]{:S(2)}) %collective-permute-start) | collective-permute-done | bytes 12320 | tf_op jit(solution)/shard_map/ppermute | solution.py:278
  8.9 2.8 %collective-permute-start.1 = (bf16[32,384]{1,0:T(8,128)(2,1)S(1)}, bf16[32,384]{1,0:T(8,128)(2,1)S(1)}, u32[]{:S(2)}, u32[]{:S(2)}) collective-permute-start(bf16[32,384]{1,0:T(8,128)(2,1)S(1)} %pad_maximum_fusion.2), channel_id=1, source_target_pairs={{0,7},{1,6},{2,5},{3,4},{4,3},{5,2},{6,1},{7,0},{8,15},{9,14},{10,... | collective-permute-start | bytes 73736 | tf_op jit(solution)/shard_map/ppermute | solution.py:278
  11.7 0.4 %collective-permute-start.2 = (bf16[32,384]{1,0:T(8,128)(2,1)S(1)}, bf16[32,384]{1,0:T(8,128)(2,1)S(1)}, u32[]{:S(2)}, u32[]{:S(2)}) collective-permute-start(bf16[32,384]{1,0:T(8,128)(2,1)S(1)} %pad_maximum_fusion.2), channel_id=1, source_target_pairs={{0,5},{1,4},{2,7},{3,6},{4,1},{5,0},{6,3},{7,2},{8,13},{9,12},{10,... | collective-permute-start | bytes 73736 | tf_op jit(solution)/shard_map/ppermute | solution.py:278
  12.1 0.2 collective-permute-start.3
  12.3 1.0 %collective-permute-done.1 = bf16[32,384]{1,0:T(8,128)(2,1)S(1)} collective-permute-done((bf16[32,384]{1,0:T(8,128)(2,1)S(1)}, bf16[32,384]{1,0:T(8,128)(2,1)S(1)}, u32[]{:S(2)}, u32[]{:S(2)}) %collective-permute-start.1) | collective-permute-done | bytes 24608 | tf_op jit(solution)/shard_map/ppermute | solution.py:278
  13.3 1.6 %collective-permute-done.2 = bf16[32,384]{1,0:T(8,128)(2,1)S(1)} collective-permute-done((bf16[32,384]{1,0:T(8,128)(2,1)S(1)}, bf16[32,384]{1,0:T(8,128)(2,1)S(1)}, u32[]{:S(2)}, u32[]{:S(2)}) %collective-permute-start.2) | collective-permute-done | bytes 24608 | tf_op jit(solution)/shard_map/ppermute | solution.py:278
  15.0 0.4 %collective-permute-done.3 = bf16[32,384]{1,0:T(8,128)(2,1)S(1)} collective-permute-done((bf16[32,384]{1,0:T(8,128)(2,1)S(1)}, bf16[32,384]{1,0:T(8,128)(2,1)S(1)}, u32[]{:S(2)}, u32[]{:S(2)}) %collective-permute-start.3) | collective-permute-done | bytes 24608 | tf_op jit(solution)/shard_map/ppermute | solution.py:278
  15.4 0.2 collective-permute-start.4
  15.6 1.2 %collective-permute-done.4 = bf16[128,384]{1,0:T(8,128)(2,1)S(1)} collective-permute-done((bf16[128,384]{1,0:T(8,128)(2,1)S(1)}, bf16[128,384]{1,0:T(8,128)(2,1)S(1)}, u32[]{:S(2)}, u32[]{:S(2)}) %collective-permute-start.4) | collective-permute-done | bytes 98336 | tf_op jit(solution)/shard_map/ppermute | solution.py:278
  16.9 9.0 %precondition.1 = bf16[16,1024]{1,0:T(8,128)(2,1)S(1)} custom-call(bf16[256,384]{1,0:T(8,128)(2,1)S(1)} %constant_dynamic-update-slice_fusion.5.tok, bf16[1024,16384]{1,0:T(8,128)(2,1)S(1)} %bitcast.3), custom_call_target="tpu_custom_call" | custom-call | flops 536870912 | bytes 33554432 | tf_op jit(solution)/shard_map/precondition/pallas_call | solution.py:168
  26.0 2.5 %collective-permute-start.5 = (bf16[1,16,1024]{2,1,0:T(8,128)(2,1)S(1)}, bf16[1,16,1024]{2,1,0:T(8,128)(2,1)S(1)}, u32[]{:S(2)}, u32[]{:S(2)}) collective-permute-start(bf16[1,16,1024]{2,1,0:T(8,128)(2,1)S(1)} %bitcast.4), channel_id=1, source_target_pairs={{0,9},{1,8},{2,11},{3,10},{4,13},{5,12},{6,15},{7,14},{8,1},{9,0},... | collective-permute-start | bytes 98312 | tf_op jit(solution)/shard_map/ppermute | solution.py:278
  28.5 1.8 %collective-permute-done.5 = bf16[1,16,1024]{2,1,0:T(8,128)(2,1)S(1)} collective-permute-done((bf16[1,16,1024]{2,1,0:T(8,128)(2,1)S(1)}, bf16[1,16,1024]{2,1,0:T(8,128)(2,1)S(1)}, u32[]{:S(2)}, u32[]{:S(2)}) %collective-permute-start.5) | collective-permute-done | bytes 32800 | tf_op jit(solution)/shard_map/ppermute | solution.py:278
  30.2 1.5 %collective-permute-start.9 = (bf16[2,16,1024]{2,1,0:T(8,128)(2,1)S(1)}, bf16[2,16,1024]{2,1,0:T(8,128)(2,1)S(1)}, u32[]{:S(2)}, u32[]{:S(2)}) collective-permute-start(bf16[2,16,1024]{2,1,0:T(8,128)(2,1)S(1)} %pad_maximum_fusion.1), channel_id=1, source_target_pairs={{0,7},{1,6},{2,5},{3,4},{4,3},{5,2},{6,1},{7,0},{8,15},{9,14},{10,... | collective-permute-start | bytes 196616 | tf_op jit(solution)/shard_map/ppermute | solution.py:278
  31.8 0.2 collective-permute-start.6
  32.0 1.3 %collective-permute-start.7 = (bf16[2,16,1024]{2,1,0:T(8,128)(2,1)S(1)}, bf16[2,16,1024]{2,1,0:T(8,128)(2,1)S(1)}, u32[]{:S(2)}, u32[]{:S(2)}) collective-permute-start(bf16[2,16,1024]{2,1,0:T(8,128)(2,1)S(1)} %pad_maximum_fusion.1), channel_id=1, source_target_pairs={{0,3},{1,2},{2,1},{3,0},{4,7},{5,6},{6,5},{7,4},{8,11},{9,10},{10,... | collective-permute-start | bytes 196616 | tf_op jit(solution)/shard_map/ppermute | solution.py:278
  33.3 1.9 %collective-permute-done.9 = bf16[2,16,1024]{2,1,0:T(8,128)(2,1)S(1)} collective-permute-done((bf16[2,16,1024]{2,1,0:T(8,128)(2,1)S(1)}, bf16[2,16,1024]{2,1,0:T(8,128)(2,1)S(1)}, u32[]{:S(2)}, u32[]{:S(2)}) %collective-permute-start.9) | collective-permute-done | bytes 65568 | tf_op jit(solution)/shard_map/ppermute | solution.py:278
  35.3 0.3 collective-permute-start.10
  35.6 1.4 %collective-permute-done.7 = bf16[2,16,1024]{2,1,0:T(8,128)(2,1)S(1)} collective-permute-done((bf16[2,16,1024]{2,1,0:T(8,128)(2,1)S(1)}, bf16[2,16,1024]{2,1,0:T(8,128)(2,1)S(1)}, u32[]{:S(2)}, u32[]{:S(2)}) %collective-permute-start.7) | collective-permute-done | bytes 65568 | tf_op jit(solution)/shard_map/ppermute | solution.py:278
  36.9 0.1 collective-permute-start.8
  37.1 0.8 %score_near.1 = (f32[16,16]{1,0:T(8,128)S(1)}, bf16[32,4096]{1,0:T(8,128)(2,1)S(1)}) custom-call(bf16[4,16,1024]{2,1,0:T(8,128)(2,1)S(1)} %pad_maximum_fusion.refs_0_, bf16[4,16,1024]{2,1,0:T(8,128)(2,1)S(1)} %constant_dynamic-update-slice_fusion.11.refs_1_, bf16[4,16,1024]{2,1,0:T(8,128)(2,1)S(1)} %collective-permute-done.10.refs_2_, ...), custom_call_target="tpu_custom_call" | custom-call | flops 12582912 | bytes 786432 | tf_op jit(solution)/shard_map/score_near/pallas_call | solution.py:232
  37.9 0.4 %collective-permute-done.8.far = bf16[4,16,1024]{2,1,0:T(8,128)(2,1)S(1)} collective-permute-done((bf16[4,16,1024]{2,1,0:T(8,128)(2,1)S(1)}, bf16[4,16,1024]{2,1,0:T(8,128)(2,1)S(1)}, u32[]{:S(2)}, u32[]{:S(2)}) %collective-permute-start.8) | collective-permute-done | bytes 131104 | tf_op jit(solution)/shard_map/ppermute | solution.py:278
  38.3 0.8 %score_far.1 = f32[16,16]{1,0:T(8,128)} custom-call(bf16[4,16,1024]{2,1,0:T(8,128)(2,1)S(1)} %collective-permute-done.8.far, f32[16,16]{1,0:T(8,128)S(1)} %get-tuple-element.7.part, bf16[32,4096]{1,0:T(8,128)(2,1)S(1)} %get-tuple-element.8.sums), custom_call_target="tpu_custom_call" | custom-call | flops 4194304 | bytes 262144 | tf_op jit(solution)/shard_map/score_far/pallas_call | solution.py:251
  (37 shorter events, 0.3 us)
Async XLA Ops:
  0.0 3.8 %copy-start.2 = (s32[16]{0:T(128)S(1)}, s32[16]{0:T(128)}, u32[]{:S(2)}) copy-start(s32[16]{0:T(128)} %param.14) | copy-start | bytes 196
  3.8 13.0 %slice-start = ((s8[33554432]{0:T(1024)(128)(4,1)}), s8[4194304]{0:T(1024)(128)(4,1)S(1)}, s32[]{:S(2)}) async-start(s8[33554432]{0:T(1024)(128)(4,1)} %bitcast.2), calls=%async_computation | async-start | bytes 8388608
  3.8 13.0 %slice-start.1 = ((s8[33554432]{0:T(1024)(128)(4,1)}), s8[4194304]{0:T(1024)(128)(4,1)S(1)}, s32[]{:S(2)}) async-start(s8[33554432]{0:T(1024)(128)(4,1)} %bitcast.2), calls=%async_computation.1 | async-start | bytes 8388608
  3.8 13.0 %slice-start.2 = ((s8[33554432]{0:T(1024)(128)(4,1)}), s8[4194304]{0:T(1024)(128)(4,1)S(1)}, s32[]{:S(2)}) async-start(s8[33554432]{0:T(1024)(128)(4,1)} %bitcast.2), calls=%async_computation.2 | async-start | bytes 8388608
  3.8 13.0 %slice-start.3 = ((s8[33554432]{0:T(1024)(128)(4,1)}), s8[4194304]{0:T(1024)(128)(4,1)S(1)}, s32[]{:S(2)}) async-start(s8[33554432]{0:T(1024)(128)(4,1)} %bitcast.2), calls=%async_computation.3 | async-start | bytes 8388608
  3.8 13.0 %slice-start.4 = ((s8[33554432]{0:T(1024)(128)(4,1)}), s8[4194304]{0:T(1024)(128)(4,1)S(1)}, s32[]{:S(2)}) async-start(s8[33554432]{0:T(1024)(128)(4,1)} %bitcast.2), calls=%async_computation.4 | async-start | bytes 8388608
  3.8 13.0 %slice-start.5 = ((s8[33554432]{0:T(1024)(128)(4,1)}), s8[4194304]{0:T(1024)(128)(4,1)S(1)}, s32[]{:S(2)}) async-start(s8[33554432]{0:T(1024)(128)(4,1)} %bitcast.2), calls=%async_computation.5 | async-start | bytes 8388608
  3.8 13.0 %slice-start.6 = ((s8[33554432]{0:T(1024)(128)(4,1)}), s8[4194304]{0:T(1024)(128)(4,1)S(1)}, s32[]{:S(2)}) async-start(s8[33554432]{0:T(1024)(128)(4,1)} %bitcast.2), calls=%async_computation.6 | async-start | bytes 8388608
  3.8 13.0 %slice-start.7 = ((s8[33554432]{0:T(1024)(128)(4,1)}), s8[4194304]{0:T(1024)(128)(4,1)S(1)}, s32[]{:S(2)}) async-start(s8[33554432]{0:T(1024)(128)(4,1)} %bitcast.2), calls=%async_computation.7 | async-start | bytes 8388608
  3.9 4.9 %collective-permute-start = (bf16[16,384]{1,0:T(8,128)(2,1)S(1)}, bf16[16,384]{1,0:T(8,128)(2,1)S(1)}, u32[]{:S(2)}, u32[]{:S(2)}) collective-permute-start(bf16[16,384]{1,0:T(8,128)(2,1)S(1)} %mark.1), channel_id=1, source_target_pairs={{0,9},{1,8},{2,11},{3,10},{4,13},{5,12},{6,15},{7,14},{8,1},{9,0},... | collective-permute-start | bytes 36872 | tf_op jit(solution)/shard_map/ppermute | solution.py:278
  8.9 4.4 %collective-permute-start.1 = (bf16[32,384]{1,0:T(8,128)(2,1)S(1)}, bf16[32,384]{1,0:T(8,128)(2,1)S(1)}, u32[]{:S(2)}, u32[]{:S(2)}) collective-permute-start(bf16[32,384]{1,0:T(8,128)(2,1)S(1)} %pad_maximum_fusion.2), channel_id=1, source_target_pairs={{0,7},{1,6},{2,5},{3,4},{4,3},{5,2},{6,1},{7,0},{8,15},{9,14},{10,... | collective-permute-start | bytes 73736 | tf_op jit(solution)/shard_map/ppermute | solution.py:278
  11.7 3.3 %collective-permute-start.2 = (bf16[32,384]{1,0:T(8,128)(2,1)S(1)}, bf16[32,384]{1,0:T(8,128)(2,1)S(1)}, u32[]{:S(2)}, u32[]{:S(2)}) collective-permute-start(bf16[32,384]{1,0:T(8,128)(2,1)S(1)} %pad_maximum_fusion.2), channel_id=1, source_target_pairs={{0,5},{1,4},{2,7},{3,6},{4,1},{5,0},{6,3},{7,2},{8,13},{9,12},{10,... | collective-permute-start | bytes 73736 | tf_op jit(solution)/shard_map/ppermute | solution.py:278
  12.1 3.3 %collective-permute-start.3 = (bf16[32,384]{1,0:T(8,128)(2,1)S(1)}, bf16[32,384]{1,0:T(8,128)(2,1)S(1)}, u32[]{:S(2)}, u32[]{:S(2)}) collective-permute-start(bf16[32,384]{1,0:T(8,128)(2,1)S(1)} %pad_maximum_fusion.2), channel_id=1, source_target_pairs={{0,3},{1,2},{2,1},{3,0},{4,7},{5,6},{6,5},{7,4},{8,11},{9,10},{10,... | collective-permute-start | bytes 73736 | tf_op jit(solution)/shard_map/ppermute | solution.py:278
  15.4 1.4 %collective-permute-start.4 = (bf16[128,384]{1,0:T(8,128)(2,1)S(1)}, bf16[128,384]{1,0:T(8,128)(2,1)S(1)}, u32[]{:S(2)}, u32[]{:S(2)}) collective-permute-start(bf16[128,384]{1,0:T(8,128)(2,1)S(1)} %get-tuple-element.9), channel_id=1, source_target_pairs={{0,1},{1,0},{2,3},{3,2},{4,5},{5,4},{6,7},{7,6},{8,9},{9,8},{10,11... | collective-permute-start | bytes 294920 | tf_op jit(solution)/shard_map/ppermute | solution.py:278
  16.9 20.2 %copy-start = (bf16[48,16384]{1,0:T(8,128)(2,1)S(1)}, bf16[48,16384]{1,0:T(8,128)(2,1)}, u32[]{:S(2)}) copy-start(bf16[48,16384]{1,0:T(8,128)(2,1)} %refs_3_.1) | copy-start | bytes 4718596
  16.9 20.2 %copy-start.1 = (s32[1,48]{1,0:T(1,128)S(1)}, s32[1,48]{1,0:T(1,128)}, u32[]{:S(2)}) copy-start(s32[1,48]{1,0:T(1,128)} %refs_4_.1) | copy-start | bytes 580
  26.0 4.3 %collective-permute-start.5 = (bf16[1,16,1024]{2,1,0:T(8,128)(2,1)S(1)}, bf16[1,16,1024]{2,1,0:T(8,128)(2,1)S(1)}, u32[]{:S(2)}, u32[]{:S(2)}) collective-permute-start(bf16[1,16,1024]{2,1,0:T(8,128)(2,1)S(1)} %bitcast.4), channel_id=1, source_target_pairs={{0,9},{1,8},{2,11},{3,10},{4,13},{5,12},{6,15},{7,14},{8,1},{9,0},... | collective-permute-start | bytes 98312 | tf_op jit(solution)/shard_map/ppermute | solution.py:278
  30.2 5.0 %collective-permute-start.9 = (bf16[2,16,1024]{2,1,0:T(8,128)(2,1)S(1)}, bf16[2,16,1024]{2,1,0:T(8,128)(2,1)S(1)}, u32[]{:S(2)}, u32[]{:S(2)}) collective-permute-start(bf16[2,16,1024]{2,1,0:T(8,128)(2,1)S(1)} %pad_maximum_fusion.1), channel_id=1, source_target_pairs={{0,7},{1,6},{2,5},{3,4},{4,3},{5,2},{6,1},{7,0},{8,15},{9,14},{10,... | collective-permute-start | bytes 196616 | tf_op jit(solution)/shard_map/ppermute | solution.py:278
  31.8 3.8 %collective-permute-start.6 = (bf16[2,16,1024]{2,1,0:T(8,128)(2,1)S(1)}, bf16[2,16,1024]{2,1,0:T(8,128)(2,1)S(1)}, u32[]{:S(2)}, u32[]{:S(2)}) collective-permute-start(bf16[2,16,1024]{2,1,0:T(8,128)(2,1)S(1)} %pad_maximum_fusion.1), channel_id=1, source_target_pairs={{0,5},{1,4},{2,7},{3,6},{4,1},{5,0},{6,3},{7,2},{8,13},{9,12},{10,... | collective-permute-start | bytes 196616 | tf_op jit(solution)/shard_map/ppermute | solution.py:278
  32.0 5.0 %collective-permute-start.7 = (bf16[2,16,1024]{2,1,0:T(8,128)(2,1)S(1)}, bf16[2,16,1024]{2,1,0:T(8,128)(2,1)S(1)}, u32[]{:S(2)}, u32[]{:S(2)}) collective-permute-start(bf16[2,16,1024]{2,1,0:T(8,128)(2,1)S(1)} %pad_maximum_fusion.1), channel_id=1, source_target_pairs={{0,3},{1,2},{2,1},{3,0},{4,7},{5,6},{6,5},{7,4},{8,11},{9,10},{10,... | collective-permute-start | bytes 196616 | tf_op jit(solution)/shard_map/ppermute | solution.py:278
  35.3 1.8 %collective-permute-start.10 = (bf16[4,16,1024]{2,1,0:T(8,128)(2,1)S(1)}, bf16[4,16,1024]{2,1,0:T(8,128)(2,1)S(1)}, u32[]{:S(2)}, u32[]{:S(2)}) collective-permute-start(bf16[4,16,1024]{2,1,0:T(8,128)(2,1)S(1)} %pad_maximum_fusion.refs_0_), channel_id=1, source_target_pairs={{0,1},{1,0},{2,3},{3,2},{4,5},{5,4},{6,7},{7,6},{8,9},{9,8},{10,11... | collective-permute-start | bytes 393224 | tf_op jit(solution)/shard_map/ppermute | solution.py:278
  36.9 1.3 %collective-permute-start.8 = (bf16[4,16,1024]{2,1,0:T(8,128)(2,1)S(1)}, bf16[4,16,1024]{2,1,0:T(8,128)(2,1)S(1)}, u32[]{:S(2)}, u32[]{:S(2)}) collective-permute-start(bf16[4,16,1024]{2,1,0:T(8,128)(2,1)S(1)} %constant_dynamic-update-slice_fusion.11.refs_1_), channel_id=1, source_target_pairs={{0,1},{1,0},{2,3},{3,2},{4,5},{5,4},{6,7},{7,6},{8,9},{9,8},{10,11... | collective-permute-start | bytes 393224 | tf_op jit(solution)/shard_map/ppermute | solution.py:278
where the time goes:
time: 39.3 us; the launch traced here: 39.1 us
  Pallas kernels  14.5 us (37%)
  starting transfers between devices  13.2 us (34%)
  waiting for transfers between devices  11.1 us (28%)
    ppermute x11, starting transfers between devices, swap(): return lax.ppermute(x, 'rows', [(i, i ^ mask) for i in range(n)])  13.2 us
    ppermute x11, waiting for transfers between devices, swap(): return lax.ppermute(x, 'rows', [(i, i ^ mask) for i in range(n)])  11.1 us
    pallas_call x1, Pallas kernels, precondition(): pl.pallas_call(functools.partial(precond_kernel, kin=kin, kout=kout, per=...  9.05 us
    pallas_call x1, Pallas kernels, project(): pl.pallas_call(functools.partial(project_kernel, steps=steps), in_specs=[...  3.75 us
    pallas_call x1, Pallas kernels, score_far(): pl.pallas_call(far_kernel, in_specs=[VMEM] * 3, out_specs=VMEM, out_shape...  0.84 us
  transfers between devices with their start and end apart: 11, of which 9 were waited for; matrix products, arithmetic and copies ran while one was open for 0% of the time, Pallas kernels for 2%

commit v1 on v0

--- a/solution.py
+++ b/solution.py
@@ -294,9 +294,15 @@
         in_acts, out_grads, in_projection, out_projection, query_ids[None, :], queries
     )
     *rounds, (last,) = rounds_of(n)
-    for masks in rounds:
+    for masks in rounds[:-1]:
         tok, _ = spread(tok, [0], masks, n)
-    tok = jnp.concatenate([tok, swap(tok, last, n)], axis=0)
+    masks = rounds[-1]
+    pieces = [swap(tok, mask, n) for mask in masks]
+    first = len(masks) // 2
+    early = jnp.concatenate([tok] + pieces[:first], axis=0)
+    late = jnp.concatenate(pieces[first:], axis=0)
+    across = swap(early, last, n)
+    tok = jnp.concatenate([early, late, across, swap(late, last, n)], axis=0)
     near, held = precondition(tok, inverse, kin, kout, queries)[None], [0]
     for masks in rounds[:-1]:
         near, held = spread(near, held, masks, n)

time: 39.3 us -> 39.2 us (level)
  waiting for transfers between devices: 11.1 us -> 10.6 us
    ppermute x11 -> x12, waiting for transfers between devices: 11.1 us -> 10.6 us  [swap(): return lax.ppermute(x, 'rows', [(i, i ^ mask) for i in range(n)])]
    ppermute x11 -> x12, starting transfers between devices: 13.2 us -> 13.5 us  [swap(): return lax.ppermute(x, 'rows', [(i, i ^ mask) for i in range(n)])]
  transfers between devices with their start and end apart: 11 -> 12, of which waited for: 9 -> 10; matrix products, arithmetic and copies ran while one was open for 0% -> 0% of each run, Pallas kernels for 2% -> 2%
where the time goes in v1:
time: 39.2 us; the launch traced here: 39 us
  Pallas kernels  14.5 us (37%)
  starting transfers between devices  13.5 us (34%)
  waiting for transfers between devices  10.6 us (27%)
    ppermute x12, starting transfers between devices, swap(): return lax.ppermute(x, 'rows', [(i, i ^ mask) for i in range(n)])  13.5 us
    ppermute x12, waiting for transfers between devices, swap(): return lax.ppermute(x, 'rows', [(i, i ^ mask) for i in range(n)])  10.6 us
    pallas_call x1, Pallas kernels, precondition(): pl.pallas_call(functools.partial(precond_kernel, kin=kin, kout=kout, per=...  9.05 us
    pallas_call x1, Pallas kernels, project(): pl.pallas_call(functools.partial(project_kernel, steps=steps), in_specs=[...  3.75 us
    pallas_call x1, Pallas kernels, score_far(): pl.pallas_call(far_kernel, in_specs=[VMEM] * 3, out_specs=VMEM, out_shape...  0.84 us
  transfers between devices with their start and end apart: 12, of which 10 were waited for; matrix products, arithmetic and copies ran while one was open for 0% of the time, Pallas kernels for 2%

profile of v1, /device:TPU:0, one launch (start us, length us, event | category | flops | bytes accessed | tf_op | source)
XLA Modules:
  0.0 39.0 jit_solution(1945450860720789373)
XLA Ops:
  0.0 3.7 %project.1.raw = bf16[16,256]{1,0:T(8,128)(2,1)S(1)} custom-call(bf16[16,14336]{1,0:T(8,128)(2,1)} %acts.1, bf16[16,4096]{1,0:T(8,128)(2,1)} %grads.1, bf16[128,14336]{1,0:T(8,128)(2,1)} %in_w.1, bf16[128,4096]{1,0:T(8,128)(2,1)} %out_w.1), custom_call_target="tpu_custom_call" | custom-call | tf_op jit(solution)/shard_map/project/pallas_call | solution.py:91
  3.9 3.5 %collective-permute-start = (bf16[16,384]{1,0:T(8,128)(2,1)S(1)}, bf16[16,384]{1,0:T(8,128)(2,1)S(1)}, u32[]{:S(2)}, u32[]{:S(2)}) collective-permute-start(bf16[16,384]{1,0:T(8,128)(2,1)S(1)} %mark.1), channel_id=1, source_target_pairs={{0,9},{1,8},{2,11},{3,10},{4,13},{5,12},{6,15},{7,14},{8,1},{9,0},... | collective-permute-start | bytes 36872 | tf_op jit(solution)/shard_map/ppermute | solution.py:278
  7.5 1.4 %collective-permute-done = bf16[16,384]{1,0:T(8,128)(2,1)S(1)} collective-permute-done((bf16[16,384]{1,0:T(8,128)(2,1)S(1)}, bf16[16,384]{1,0:T(8,128)(2,1)S(1)}, u32[]{:S(2)}, u32[]{:S(2)}) %collective-permute-start) | collective-permute-done | bytes 12320 | tf_op jit(solution)/shard_map/ppermute | solution.py:278
  8.9 2.8 %collective-permute-start.1 = (bf16[32,384]{1,0:T(8,128)(2,1)S(1)}, bf16[32,384]{1,0:T(8,128)(2,1)S(1)}, u32[]{:S(2)}, u32[]{:S(2)}) collective-permute-start(bf16[32,384]{1,0:T(8,128)(2,1)S(1)} %pad_maximum_fusion.4), channel_id=1, source_target_pairs={{0,7},{1,6},{2,5},{3,4},{4,3},{5,2},{6,1},{7,0},{8,15},{9,14},{10,... | collective-permute-start | bytes 73736 | tf_op jit(solution)/shard_map/ppermute | solution.py:278
  11.7 0.4 %collective-permute-start.2 = (bf16[32,384]{1,0:T(8,128)(2,1)S(1)}, bf16[32,384]{1,0:T(8,128)(2,1)S(1)}, u32[]{:S(2)}, u32[]{:S(2)}) collective-permute-start(bf16[32,384]{1,0:T(8,128)(2,1)S(1)} %pad_maximum_fusion.4), channel_id=1, source_target_pairs={{0,5},{1,4},{2,7},{3,6},{4,1},{5,0},{6,3},{7,2},{8,13},{9,12},{10,... | collective-permute-start | bytes 73736 | tf_op jit(solution)/shard_map/ppermute | solution.py:278
  12.3 1.0 %collective-permute-done.1 = bf16[32,384]{1,0:T(8,128)(2,1)S(1)} collective-permute-done((bf16[32,384]{1,0:T(8,128)(2,1)S(1)}, bf16[32,384]{1,0:T(8,128)(2,1)S(1)}, u32[]{:S(2)}, u32[]{:S(2)}) %collective-permute-start.1) | collective-permute-done | bytes 24608 | tf_op jit(solution)/shard_map/ppermute | solution.py:278
  13.3 0.4 collective-permute-start.4
  13.7 1.3 %collective-permute-done.2 = bf16[32,384]{1,0:T(8,128)(2,1)S(1)} collective-permute-done((bf16[32,384]{1,0:T(8,128)(2,1)S(1)}, bf16[32,384]{1,0:T(8,128)(2,1)S(1)}, u32[]{:S(2)}, u32[]{:S(2)}) %collective-permute-start.2) | collective-permute-done | bytes 24608 | tf_op jit(solution)/shard_map/ppermute | solution.py:278
  15.0 0.4 %collective-permute-done.3 = bf16[32,384]{1,0:T(8,128)(2,1)S(1)} collective-permute-done((bf16[32,384]{1,0:T(8,128)(2,1)S(1)}, bf16[32,384]{1,0:T(8,128)(2,1)S(1)}, u32[]{:S(2)}, u32[]{:S(2)}) %collective-permute-start.3) | collective-permute-done | bytes 24608 | tf_op jit(solution)/shard_map/ppermute | solution.py:278
  15.4 0.2 collective-permute-start.5
  15.7 1.0 %collective-permute-done.5 = bf16[64,384]{1,0:T(8,128)(2,1)S(1)} collective-permute-done((bf16[64,384]{1,0:T(8,128)(2,1)S(1)}, bf16[64,384]{1,0:T(8,128)(2,1)S(1)}, u32[]{:S(2)}, u32[]{:S(2)}) %collective-permute-start.5) | collective-permute-done | bytes 49184 | tf_op jit(solution)/shard_map/ppermute | solution.py:278
  16.8 9.0 %precondition.1 = bf16[16,1024]{1,0:T(8,128)(2,1)S(1)} custom-call(bf16[256,384]{1,0:T(8,128)(2,1)S(1)} %constant_dynamic-update-slice_fusion.tok, bf16[1024,16384]{1,0:T(8,128)(2,1)S(1)} %bitcast.3), custom_call_target="tpu_custom_call" | custom-call | flops 536870912 | bytes 33554432 | tf_op jit(solution)/shard_map/precondition/pallas_call | solution.py:168
  25.8 2.5 %collective-permute-start.6 = (bf16[1,16,1024]{2,1,0:T(8,128)(2,1)S(1)}, bf16[1,16,1024]{2,1,0:T(8,128)(2,1)S(1)}, u32[]{:S(2)}, u32[]{:S(2)}) collective-permute-start(bf16[1,16,1024]{2,1,0:T(8,128)(2,1)S(1)} %bitcast.4), channel_id=1, source_target_pairs={{0,9},{1,8},{2,11},{3,10},{4,13},{5,12},{6,15},{7,14},{8,1},{9,0},... | collective-permute-start | bytes 98312 | tf_op jit(solution)/shard_map/ppermute | solution.py:278
  28.3 1.7 %collective-permute-done.6 = bf16[1,16,1024]{2,1,0:T(8,128)(2,1)S(1)} collective-permute-done((bf16[1,16,1024]{2,1,0:T(8,128)(2,1)S(1)}, bf16[1,16,1024]{2,1,0:T(8,128)(2,1)S(1)}, u32[]{:S(2)}, u32[]{:S(2)}) %collective-permute-start.6) | collective-permute-done | bytes 32800 | tf_op jit(solution)/shard_map/ppermute | solution.py:278
  30.1 1.5 %collective-permute-start.10 = (bf16[2,16,1024]{2,1,0:T(8,128)(2,1)S(1)}, bf16[2,16,1024]{2,1,0:T(8,128)(2,1)S(1)}, u32[]{:S(2)}, u32[]{:S(2)}) collective-permute-start(bf16[2,16,1024]{2,1,0:T(8,128)(2,1)S(1)} %pad_maximum_fusion.1), channel_id=1, source_target_pairs={{0,7},{1,6},{2,5},{3,4},{4,3},{5,2},{6,1},{7,0},{8,15},{9,14},{10,... | collective-permute-start | bytes 196616 | tf_op jit(solution)/shard_map/ppermute | solution.py:278
  31.6 0.5 %collective-permute-start.7 = (bf16[2,16,1024]{2,1,0:T(8,128)(2,1)S(1)}, bf16[2,16,1024]{2,1,0:T(8,128)(2,1)S(1)}, u32[]{:S(2)}, u32[]{:S(2)}) collective-permute-start(bf16[2,16,1024]{2,1,0:T(8,128)(2,1)S(1)} %pad_maximum_fusion.1), channel_id=1, source_target_pairs={{0,5},{1,4},{2,7},{3,6},{4,1},{5,0},{6,3},{7,2},{8,13},{9,12},{10,... | collective-permute-start | bytes 196616 | tf_op jit(solution)/shard_map/ppermute | solution.py:278
  32.1 1.1 %collective-permute-start.8 = (bf16[2,16,1024]{2,1,0:T(8,128)(2,1)S(1)}, bf16[2,16,1024]{2,1,0:T(8,128)(2,1)S(1)}, u32[]{:S(2)}, u32[]{:S(2)}) collective-permute-start(bf16[2,16,1024]{2,1,0:T(8,128)(2,1)S(1)} %pad_maximum_fusion.1), channel_id=1, source_target_pairs={{0,3},{1,2},{2,1},{3,0},{4,7},{5,6},{6,5},{7,4},{8,11},{9,10},{10,... | collective-permute-start | bytes 196616 | tf_op jit(solution)/shard_map/ppermute | solution.py:278
  33.2 1.9 %collective-permute-done.10 = bf16[2,16,1024]{2,1,0:T(8,128)(2,1)S(1)} collective-permute-done((bf16[2,16,1024]{2,1,0:T(8,128)(2,1)S(1)}, bf16[2,16,1024]{2,1,0:T(8,128)(2,1)S(1)}, u32[]{:S(2)}, u32[]{:S(2)}) %collective-permute-start.10) | collective-permute-done | bytes 65568 | tf_op jit(solution)/shard_map/ppermute | solution.py:278
  35.1 0.3 collective-permute-start.11
  35.4 0.3 collective-permute-done.7
  35.7 1.2 %collective-permute-done.8 = bf16[2,16,1024]{2,1,0:T(8,128)(2,1)S(1)} collective-permute-done((bf16[2,16,1024]{2,1,0:T(8,128)(2,1)S(1)}, bf16[2,16,1024]{2,1,0:T(8,128)(2,1)S(1)}, u32[]{:S(2)}, u32[]{:S(2)}) %collective-permute-start.8) | collective-permute-done | bytes 65568 | tf_op jit(solution)/shard_map/ppermute | solution.py:278
  37.0 0.8 %score_near.1 = (f32[16,16]{1,0:T(8,128)S(1)}, bf16[32,4096]{1,0:T(8,128)(2,1)S(1)}) custom-call(bf16[4,16,1024]{2,1,0:T(8,128)(2,1)S(1)} %pad_maximum_fusion.refs_0_, bf16[4,16,1024]{2,1,0:T(8,128)(2,1)S(1)} %constant_dynamic-update-slice_fusion.7.refs_1_, bf16[4,16,1024]{2,1,0:T(8,128)(2,1)S(1)} %collective-permute-done.11.refs_2_, ...), custom_call_target="tpu_custom_call" | custom-call | flops 12582912 | bytes 786432 | tf_op jit(solution)/shard_map/score_near/pallas_call | solution.py:232
  37.7 0.4 %collective-permute-done.9.far = bf16[4,16,1024]{2,1,0:T(8,128)(2,1)S(1)} collective-permute-done((bf16[4,16,1024]{2,1,0:T(8,128)(2,1)S(1)}, bf16[4,16,1024]{2,1,0:T(8,128)(2,1)S(1)}, u32[]{:S(2)}, u32[]{:S(2)}) %collective-permute-start.9) | collective-permute-done | bytes 131104 | tf_op jit(solution)/shard_map/ppermute | solution.py:278
  38.2 0.8 %score_far.1 = f32[16,16]{1,0:T(8,128)} custom-call(bf16[4,16,1024]{2,1,0:T(8,128)(2,1)S(1)} %collective-permute-done.9.far, f32[16,16]{1,0:T(8,128)S(1)} %get-tuple-element.7.part, bf16[32,4096]{1,0:T(8,128)(2,1)S(1)} %get-tuple-element.8.sums), custom_call_target="tpu_custom_call" | custom-call | flops 4194304 | bytes 262144 | tf_op jit(solution)/shard_map/score_far/pallas_call | solution.py:251
  (42 shorter events, 0.6 us)
Async XLA Ops:
  0.0 3.8 %copy-start.2 = (s32[16]{0:T(128)S(1)}, s32[16]{0:T(128)}, u32[]{:S(2)}) copy-start(s32[16]{0:T(128)} %param.14) | copy-start | bytes 196
  3.8 12.9 %slice-start = ((s8[33554432]{0:T(1024)(128)(4,1)}), s8[4194304]{0:T(1024)(128)(4,1)S(1)}, s32[]{:S(2)}) async-start(s8[33554432]{0:T(1024)(128)(4,1)} %bitcast.2), calls=%async_computation | async-start | bytes 8388608
  3.8 12.9 %slice-start.1 = ((s8[33554432]{0:T(1024)(128)(4,1)}), s8[4194304]{0:T(1024)(128)(4,1)S(1)}, s32[]{:S(2)}) async-start(s8[33554432]{0:T(1024)(128)(4,1)} %bitcast.2), calls=%async_computation.1 | async-start | bytes 8388608
  3.8 12.9 %slice-start.2 = ((s8[33554432]{0:T(1024)(128)(4,1)}), s8[4194304]{0:T(1024)(128)(4,1)S(1)}, s32[]{:S(2)}) async-start(s8[33554432]{0:T(1024)(128)(4,1)} %bitcast.2), calls=%async_computation.2 | async-start | bytes 8388608
  3.8 12.9 %slice-start.3 = ((s8[33554432]{0:T(1024)(128)(4,1)}), s8[4194304]{0:T(1024)(128)(4,1)S(1)}, s32[]{:S(2)}) async-start(s8[33554432]{0:T(1024)(128)(4,1)} %bitcast.2), calls=%async_computation.3 | async-start | bytes 8388608
  3.8 12.9 %slice-start.4 = ((s8[33554432]{0:T(1024)(128)(4,1)}), s8[4194304]{0:T(1024)(128)(4,1)S(1)}, s32[]{:S(2)}) async-start(s8[33554432]{0:T(1024)(128)(4,1)} %bitcast.2), calls=%async_computation.4 | async-start | bytes 8388608
  3.8 12.9 %slice-start.5 = ((s8[33554432]{0:T(1024)(128)(4,1)}), s8[4194304]{0:T(1024)(128)(4,1)S(1)}, s32[]{:S(2)}) async-start(s8[33554432]{0:T(1024)(128)(4,1)} %bitcast.2), calls=%async_computation.5 | async-start | bytes 8388608
  3.8 12.9 %slice-start.6 = ((s8[33554432]{0:T(1024)(128)(4,1)}), s8[4194304]{0:T(1024)(128)(4,1)S(1)}, s32[]{:S(2)}) async-start(s8[33554432]{0:T(1024)(128)(4,1)} %bitcast.2), calls=%async_computation.6 | async-start | bytes 8388608
  3.8 12.9 %slice-start.7 = ((s8[33554432]{0:T(1024)(128)(4,1)}), s8[4194304]{0:T(1024)(128)(4,1)S(1)}, s32[]{:S(2)}) async-start(s8[33554432]{0:T(1024)(128)(4,1)} %bitcast.2), calls=%async_computation.7 | async-start | bytes 8388608
  3.9 4.9 %collective-permute-start = (bf16[16,384]{1,0:T(8,128)(2,1)S(1)}, bf16[16,384]{1,0:T(8,128)(2,1)S(1)}, u32[]{:S(2)}, u32[]{:S(2)}) collective-permute-start(bf16[16,384]{1,0:T(8,128)(2,1)S(1)} %mark.1), channel_id=1, source_target_pairs={{0,9},{1,8},{2,11},{3,10},{4,13},{5,12},{6,15},{7,14},{8,1},{9,0},... | collective-permute-start | bytes 36872 | tf_op jit(solution)/shard_map/ppermute | solution.py:278
  8.9 4.4 %collective-permute-start.1 = (bf16[32,384]{1,0:T(8,128)(2,1)S(1)}, bf16[32,384]{1,0:T(8,128)(2,1)S(1)}, u32[]{:S(2)}, u32[]{:S(2)}) collective-permute-start(bf16[32,384]{1,0:T(8,128)(2,1)S(1)} %pad_maximum_fusion.4), channel_id=1, source_target_pairs={{0,7},{1,6},{2,5},{3,4},{4,3},{5,2},{6,1},{7,0},{8,15},{9,14},{10,... | collective-permute-start | bytes 73736 | tf_op jit(solution)/shard_map/ppermute | solution.py:278
  11.7 3.3 %collective-permute-start.2 = (bf16[32,384]{1,0:T(8,128)(2,1)S(1)}, bf16[32,384]{1,0:T(8,128)(2,1)S(1)}, u32[]{:S(2)}, u32[]{:S(2)}) collective-permute-start(bf16[32,384]{1,0:T(8,128)(2,1)S(1)} %pad_maximum_fusion.4), channel_id=1, source_target_pairs={{0,5},{1,4},{2,7},{3,6},{4,1},{5,0},{6,3},{7,2},{8,13},{9,12},{10,... | collective-permute-start | bytes 73736 | tf_op jit(solution)/shard_map/ppermute | solution.py:278
  12.1 3.3 %collective-permute-start.3 = (bf16[32,384]{1,0:T(8,128)(2,1)S(1)}, bf16[32,384]{1,0:T(8,128)(2,1)S(1)}, u32[]{:S(2)}, u32[]{:S(2)}) collective-permute-start(bf16[32,384]{1,0:T(8,128)(2,1)S(1)} %pad_maximum_fusion.4), channel_id=1, source_target_pairs={{0,3},{1,2},{2,1},{3,0},{4,7},{5,6},{6,5},{7,4},{8,11},{9,10},{10,... | collective-permute-start | bytes 73736 | tf_op jit(solution)/shard_map/ppermute | solution.py:278
  13.3 2.3 %collective-permute-start.4 = (bf16[64,384]{1,0:T(8,128)(2,1)S(1)}, bf16[64,384]{1,0:T(8,128)(2,1)S(1)}, u32[]{:S(2)}, u32[]{:S(2)}) collective-permute-start(bf16[64,384]{1,0:T(8,128)(2,1)S(1)} %pad_maximum_fusion.2), channel_id=1, source_target_pairs={{0,1},{1,0},{2,3},{3,2},{4,5},{5,4},{6,7},{7,6},{8,9},{9,8},{10,11... | collective-permute-start | bytes 147464 | tf_op jit(solution)/shard_map/ppermute | solution.py:278
  15.4 1.2 %collective-permute-start.5 = (bf16[64,384]{1,0:T(8,128)(2,1)S(1)}, bf16[64,384]{1,0:T(8,128)(2,1)S(1)}, u32[]{:S(2)}, u32[]{:S(2)}) collective-permute-start(bf16[64,384]{1,0:T(8,128)(2,1)S(1)} %pad_maximum_fusion.3), channel_id=1, source_target_pairs={{0,1},{1,0},{2,3},{3,2},{4,5},{5,4},{6,7},{7,6},{8,9},{9,8},{10,11... | collective-permute-start | bytes 147464 | tf_op jit(solution)/shard_map/ppermute | solution.py:278
  16.7 20.2 %copy-start = (bf16[48,16384]{1,0:T(8,128)(2,1)S(1)}, bf16[48,16384]{1,0:T(8,128)(2,1)}, u32[]{:S(2)}) copy-start(bf16[48,16384]{1,0:T(8,128)(2,1)} %refs_3_.1) | copy-start | bytes 4718596
  16.8 20.2 %copy-start.1 = (s32[1,48]{1,0:T(1,128)S(1)}, s32[1,48]{1,0:T(1,128)}, u32[]{:S(2)}) copy-start(s32[1,48]{1,0:T(1,128)} %refs_4_.1) | copy-start | bytes 580
  25.8 4.3 %collective-permute-start.6 = (bf16[1,16,1024]{2,1,0:T(8,128)(2,1)S(1)}, bf16[1,16,1024]{2,1,0:T(8,128)(2,1)S(1)}, u32[]{:S(2)}, u32[]{:S(2)}) collective-permute-start(bf16[1,16,1024]{2,1,0:T(8,128)(2,1)S(1)} %bitcast.4), channel_id=1, source_target_pairs={{0,9},{1,8},{2,11},{3,10},{4,13},{5,12},{6,15},{7,14},{8,1},{9,0},... | collective-permute-start | bytes 98312 | tf_op jit(solution)/shard_map/ppermute | solution.py:278
  30.1 5.0 %collective-permute-start.10 = (bf16[2,16,1024]{2,1,0:T(8,128)(2,1)S(1)}, bf16[2,16,1024]{2,1,0:T(8,128)(2,1)S(1)}, u32[]{:S(2)}, u32[]{:S(2)}) collective-permute-start(bf16[2,16,1024]{2,1,0:T(8,128)(2,1)S(1)} %pad_maximum_fusion.1), channel_id=1, source_target_pairs={{0,7},{1,6},{2,5},{3,4},{4,3},{5,2},{6,1},{7,0},{8,15},{9,14},{10,... | collective-permute-start | bytes 196616 | tf_op jit(solution)/shard_map/ppermute | solution.py:278
  31.6 4.0 %collective-permute-start.7 = (bf16[2,16,1024]{2,1,0:T(8,128)(2,1)S(1)}, bf16[2,16,1024]{2,1,0:T(8,128)(2,1)S(1)}, u32[]{:S(2)}, u32[]{:S(2)}) collective-permute-start(bf16[2,16,1024]{2,1,0:T(8,128)(2,1)S(1)} %pad_maximum_fusion.1), channel_id=1, source_target_pairs={{0,5},{1,4},{2,7},{3,6},{4,1},{5,0},{6,3},{7,2},{8,13},{9,12},{10,... | collective-permute-start | bytes 196616 | tf_op jit(solution)/shard_map/ppermute | solution.py:278
  32.1 4.7 %collective-permute-start.8 = (bf16[2,16,1024]{2,1,0:T(8,128)(2,1)S(1)}, bf16[2,16,1024]{2,1,0:T(8,128)(2,1)S(1)}, u32[]{:S(2)}, u32[]{:S(2)}) collective-permute-start(bf16[2,16,1024]{2,1,0:T(8,128)(2,1)S(1)} %pad_maximum_fusion.1), channel_id=1, source_target_pairs={{0,3},{1,2},{2,1},{3,0},{4,7},{5,6},{6,5},{7,4},{8,11},{9,10},{10,... | collective-permute-start | bytes 196616 | tf_op jit(solution)/shard_map/ppermute | solution.py:278
  35.1 1.8 %collective-permute-start.11 = (bf16[4,16,1024]{2,1,0:T(8,128)(2,1)S(1)}, bf16[4,16,1024]{2,1,0:T(8,128)(2,1)S(1)}, u32[]{:S(2)}, u32[]{:S(2)}) collective-permute-start(bf16[4,16,1024]{2,1,0:T(8,128)(2,1)S(1)} %pad_maximum_fusion.refs_0_), channel_id=1, source_target_pairs={{0,1},{1,0},{2,3},{3,2},{4,5},{5,4},{6,7},{7,6},{8,9},{9,8},{10,11... | collective-permute-start | bytes 393224 | tf_op jit(solution)/shard_map/ppermute | solution.py:278
  36.8 1.3 %collective-permute-start.9 = (bf16[4,16,1024]{2,1,0:T(8,128)(2,1)S(1)}, bf16[4,16,1024]{2,1,0:T(8,128)(2,1)S(1)}, u32[]{:S(2)}, u32[]{:S(2)}) collective-permute-start(bf16[4,16,1024]{2,1,0:T(8,128)(2,1)S(1)} %constant_dynamic-update-slice_fusion.7.refs_1_), channel_id=1, source_target_pairs={{0,1},{1,0},{2,3},{3,2},{4,5},{5,4},{6,7},{7,6},{8,9},{9,8},{10,11... | collective-permute-start | bytes 393224 | tf_op jit(solution)/shard_map/ppermute | solution.py:278
